TPU v7x, 32 devices: a whole 2x2x4 slice. The times are simulated.
32 devices in a mesh: groups: 2 (over y), prompt: 4 (over z), enc: 4 (over x, core).
Axes of the slice: x: 2, y: 2, z: 4, core: 2. Of those that a mesh axis runs over, the one named last changes fastest.
Arguments:
- embed: bfloat16 [8192, 256], P(('groups', 'prompt', 'enc')), parts along dimension 0, may hold values from -4000 to 4000
- coords: int32 [64, 6], P(('groups', 'prompt')), parts along dimension 0, may hold values from 0 to 1023
- targets: int32 [64], P(('groups', 'prompt')), parts along dimension 0, may hold values from 0 to 7
- counts: int32 [4], replicated, may hold values from 1 to 8, 16 in all
- labels: int32 [512, 256], P('groups'), parts along dimension 0, may hold values from 0 to 7
- type_embed: float32 [4, 256], replicated, may hold values from -5 to 5
- fourier: float32 [2, 128], replicated, may hold values from -5 to 5
- wq_t: bfloat16 [256, 128], replicated, may hold values from -0.375 to 0.375
- wk_t: bfloat16 [256, 128], replicated, may hold values from -0.375 to 0.375
- wv_t: bfloat16 [256, 128], replicated, may hold values from -0.375 to 0.375
- wo_t: bfloat16 [128, 256], replicated, may hold values from -0.5 to 0.5
- wq_i: bfloat16 [256, 128], replicated, may hold values from -0.375 to 0.375
- wk_i: bfloat16 [256, 128], replicated, may hold values from -0.375 to 0.375
- wv_i: bfloat16 [256, 128], replicated, may hold values from -0.375 to 0.375
- wo_i: bfloat16 [128, 256], replicated, may hold values from -0.5 to 0.5
- gain_one: float32 [256], replicated, may hold values from 0.1 to 1.9
- gain_two: float32 [256], replicated, may hold values from 0.1 to 1.9
- gain_three: float32 [64], replicated, may hold values from 0.1 to 1.9
- up_one: bfloat16 [256, 256], replicated, may hold values from -0.375 to 0.375
- second_upsample_weight: bfloat16 [64, 128], replicated, may hold values from -0.75 to 0.75
- hyper_one: bfloat16 [256, 256], replicated, may hold values from -0.375 to 0.375
- hyper_two: bfloat16 [256, 32], replicated, may hold values from -0.375 to 0.375
Outputs:
- grad_embed: float32 [8192, 256], P(('groups', 'prompt', 'enc')), parts along dimension 0
There are 2 independent parts, one for each index of `groups`. A program takes and returns all parts, laid end to end along the dimension named above; an argument that names none is the same for every part. Nothing has to cross between parts.
Inputs may be any that keep to these rules, and one draw needn't show every extreme that they name: Prompt index p has counts[p] live prompts, in its first slots; the counts sum to 16 and the largest is 8.
All inputs are finite; a program needn't handle non-finite values.
Results may differ from a plain program's by a relative error of at most 0.0035.
Values may be sent and summed in bfloat16 or wider, within the bound.
No kernel may reach another device: no remote copies, remote signals or barrier semaphores. Data moves between devices by JAX's collectives and lax.ppermute only.
A program may use at most 128 MiB of HBM per device.

v0:
```python
import math

import jax
import jax.numpy as jnp
from jax import lax
from jax.sharding import PartitionSpec as P

HEADS = 8
HD = 16
IMG = 1024


highest_value = lax.Precision.HIGHEST
epsilon = 1e-05


def joined(array, axis, combine):
    everything = jax.tree.map(lambda part: lax.all_gather(part, axis), array)
    leading = jax.tree.map(lambda part: part[0], everything)

    def step(k, so_far):
        return combine(so_far, jax.tree.map(lambda part: part[k], everything))

    return lax.fori_loop(1, lax.axis_size(axis), step, leading)


def layer_norm(values, gain):
    centered = values - jnp.mean(values, axis=-1, keepdims=True)
    variance = jnp.mean(centered * centered, axis=-1, keepdims=True)
    return centered * lax.rsqrt(variance + epsilon) * gain


def fourier_code(pixel_pair, fourier):
    scaled = 2.0 * ((pixel_pair.astype(jnp.float32) + 0.5) / IMG) - 1.0
    angles = 2.0 * math.pi * jnp.dot(scaled, fourier, precision=highest_value)
    return jnp.concatenate([jnp.sin(angles), jnp.cos(angles)], axis=-1)


def prompt_tokens(corner_rows, type_embed, fourier):
    point_code = fourier_code(corner_rows[..., 0:2], fourier) + type_embed[1]
    first_code = fourier_code(corner_rows[..., 2:4], fourier) + type_embed[2]
    second_code = fourier_code(corner_rows[..., 4:6], fourier) + type_embed[3]
    output_token = jnp.broadcast_to(type_embed[0], point_code.shape)
    return jnp.stack([output_token, point_code, first_code, second_code], axis=-2)


def token_pixel_scores(labels):
    side = labels.shape[0] // 4
    grid_view = labels.reshape(side, 2, 2, side, 2, 2)
    grid_view = jnp.transpose(grid_view, (0, 3, 1, 4, 2, 5))
    return grid_view.reshape(side * side, 4, 4)


def combine_parts(first, second_result):
    top_first, first_running_total, accum_first = first
    top_second, total_second, accum_second = second_result
    top_both = jnp.maximum(top_first, top_second)
    factor_first = jnp.exp(top_first - top_both)
    factor_second = jnp.exp(top_second - top_both)
    total_both = first_running_total * factor_first + total_second * factor_second
    accum_both = accum_first * factor_first[..., None] + accum_second * factor_second[..., None]
    return (top_both, total_both, accum_both)


def image_side(query_image, image_float, tokens_one, truth, live_flag, side_weights):
    wk_i, wv_i, wo_i, gain_two, up_one, gain_three, second_upsample_weight, hyper_one, hyper_two = (
        side_weights
    )
    head_scale = HD ** (-0.5)
    row_count = query_image.shape[0]
    token_keys = jnp.dot(tokens_one, wk_i.astype(jnp.float32), precision=highest_value).reshape(
        -1, HEADS, HD
    )
    token_values = jnp.dot(tokens_one, wv_i.astype(jnp.float32), precision=highest_value).reshape(
        -1, HEADS, HD
    )
    scores = (
        jnp.einsum(
            "jhd,rhd->jhr",
            query_image.reshape(row_count, HEADS, HD),
            token_keys,
            precision=highest_value,
        )
        * head_scale
    )
    attention = jax.nn.softmax(scores, axis=-1)
    mixed = (
        jnp.einsum("jhr,rhd->jhd", attention, token_values, precision=highest_value)
        .reshape(row_count, -1)
        .astype(jnp.bfloat16)
    )
    update = jnp.dot(mixed, wo_i, preferred_element_type=jnp.float32)
    image_one = layer_norm(image_float + update, gain_two).astype(jnp.bfloat16)
    lifted = jnp.dot(image_one, up_one, preferred_element_type=jnp.float32).reshape(
        row_count, 4, -1
    )
    first_activation = jax.nn.gelu(layer_norm(lifted, gain_three), approximate=False).astype(
        jnp.bfloat16
    )
    second_result = jnp.einsum(
        "oij,jp->oip", first_activation, second_upsample_weight, preferred_element_type=jnp.float32
    )
    features = jax.nn.gelu(second_result, approximate=False).reshape(row_count, 4, 4, -1)
    hidden = jax.nn.relu(
        jnp.dot(tokens_one[0], hyper_one.astype(jnp.float32), precision=highest_value)
    )
    hyper = jnp.dot(hidden, hyper_two.astype(jnp.float32), precision=highest_value)
    logits = jnp.einsum("tasc,c->tas", features, hyper, precision=highest_value)
    losses = jax.nn.softplus(logits) - truth * logits
    return jnp.sum(losses) * live_flag * 0.25


def on_device(
    embed,
    coords,
    targets,
    counts,
    labels,
    type_embed,
    fourier,
    wq_t,
    wk_t,
    wv_t,
    wo_t,
    wq_i,
    wk_i,
    wv_i,
    wo_i,
    gain_one,
    gain_two,
    gain_three,
    up_one,
    second_upsample_weight,
    hyper_one,
    hyper_two,
):
    prompt_count = lax.axis_size("prompt")
    enc_count = lax.axis_size("enc")
    prompt_place = lax.axis_index("prompt")
    enc_place = lax.axis_index("enc")
    block_rows = embed.shape[0]
    slot_count = coords.shape[0]
    head_scale = HD ** (-0.5)
    image = lax.all_gather(embed, "prompt", axis=0, tiled=True)
    image_float = image.astype(jnp.float32)
    key_image = jnp.dot(image, wk_t, preferred_element_type=jnp.float32)
    value_image = jnp.dot(image, wv_t, preferred_element_type=jnp.float32)
    query_image = jnp.dot(image, wq_i, preferred_element_type=jnp.float32)
    local_rows = image.shape[0]
    pixel_all = token_pixel_scores(labels).reshape(prompt_count, enc_count, block_rows, 4, 4)
    own_pixels = lax.dynamic_index_in_dim(pixel_all, enc_place, axis=1, keepdims=False).reshape(
        local_rows, 4, 4
    )
    own_count = jnp.take(counts, prompt_place)
    live_flags = (jnp.arange(slot_count, dtype=jnp.int32) < own_count).astype(jnp.float32)
    tokens_zero = prompt_tokens(coords, type_embed, fourier)
    prompt_number = tokens_zero.shape[0]
    flat_tokens = tokens_zero.reshape(prompt_number * 4, -1)
    queries = jnp.dot(flat_tokens, wq_t.astype(jnp.float32), precision=highest_value).reshape(
        -1, HEADS, HD
    )
    key_heads = key_image.reshape(local_rows, HEADS, HD)
    value_heads = value_image.reshape(local_rows, HEADS, HD)
    scores = jnp.einsum("rhd,jhd->rhj", queries, key_heads, precision=highest_value) * head_scale
    local_top = jnp.max(scores, axis=-1)
    shifted = jnp.exp(scores - local_top[..., None])
    local_total = jnp.sum(shifted, axis=-1)
    local_accum = jnp.einsum("rhj,jhd->rhd", shifted, value_heads, precision=highest_value)
    global_top, global_total, global_accum = joined(
        (local_top, local_total, local_accum), "enc", combine_parts
    )
    gathered = global_accum / global_total[..., None]
    wo_t_float = wo_t.astype(jnp.float32)
    update = jnp.dot(gathered.reshape(prompt_number * 4, -1), wo_t_float, precision=highest_value)

    def token_norm(values):
        return layer_norm(values, gain_one)

    tokens_one, norm_pull = jax.vjp(token_norm, flat_tokens + update)
    side_weights = (
        wk_i,
        wv_i,
        wo_i,
        gain_two,
        up_one,
        gain_three,
        second_upsample_weight,
        hyper_one,
        hyper_two,
    )

    def single_prompt(carry, inputs):
        tokens_row, target, live_flag = inputs
        truth = (own_pixels == target).astype(jnp.float32)

        def loss_of(query_arg, image_arg, tokens_arg):
            return image_side(query_arg, image_arg, tokens_arg, truth, live_flag, side_weights)

        _, pullback = jax.vjp(loss_of, query_image, image_float, tokens_row)
        d_query, d_image, d_tokens = pullback(jnp.ones((), jnp.float32))
        return ((carry[0] + d_query, carry[1] + d_image), d_tokens)

    initial = (jnp.zeros_like(query_image), jnp.zeros_like(image_float))
    sums, token_parts = lax.scan(
        single_prompt, initial, (tokens_one.reshape(prompt_number, 4, -1), targets, live_flags)
    )
    query_grad, image_grad = sums
    token_grad = lax.psum(token_parts, "enc")
    (d_residual,) = norm_pull(token_grad.reshape(prompt_number * 4, -1))
    d_gathered = jnp.dot(d_residual, wo_t_float.T, precision=highest_value).reshape(-1, HEADS, HD)
    probs = jnp.exp(scores - global_top[..., None]) / global_total[..., None]
    d_probs = jnp.einsum("rhd,jhd->rhj", d_gathered, value_heads, precision=highest_value)
    delta_term = jnp.sum(d_gathered * gathered, axis=-1)
    d_scores = probs * (d_probs - delta_term[..., None]) * head_scale
    key_grad = jnp.einsum("rhj,rhd->jhd", d_scores, queries, precision=highest_value).reshape(
        local_rows, -1
    )
    value_grad = jnp.einsum("rhj,rhd->jhd", probs, d_gathered, precision=highest_value).reshape(
        local_rows, -1
    )
    wq_i_float = wq_i.astype(jnp.float32)
    wk_t_float = wk_t.astype(jnp.float32)
    wv_t_float = wv_t.astype(jnp.float32)
    result = image_grad
    result = result + jnp.dot(query_grad, wq_i_float.T, precision=highest_value)
    result = result + jnp.dot(key_grad, wk_t_float.T, precision=highest_value)
    result = result + jnp.dot(value_grad, wv_t_float.T, precision=highest_value)
    summed = lax.psum(result, "prompt")
    grad_embed = lax.dynamic_slice_in_dim(summed, prompt_place * block_rows, block_rows, 0)
    return grad_embed


def solution(mesh):
    in_specs = (
        P(("groups", "prompt", "enc"), None),
        P(("groups", "prompt"), None),
        P(("groups", "prompt")),
        P(),
        P("groups", None),
        P(),
        P(),
        P(),
        P(),
        P(),
        P(),
        P(),
        P(),
        P(),
        P(),
        P(),
        P(),
        P(),
        P(),
        P(),
        P(),
        P(),
    )
    out_specs = P(("groups", "prompt", "enc"), None)
    return jax.shard_map(
        on_device, mesh=mesh, in_specs=in_specs, out_specs=out_specs, check_vma=False
    )
```

profile of v0, /device:TPU:0, one launch (start us, length us, event | category | flops | bytes accessed | tf_op | source)
XLA Modules:
  0.0 566.2 jit_solution(3963014833679820841)
XLA Ops:
  12.3 17.4 %all_gather.21 = bf16[1024,256]{0,1:T(8,128)(2,1)S(1)} all-gather(bf16[256,256]{0,1:T(8,128)(2,1)S(1)} %copy.50), channel_id=1, replica_groups=mesh['groups'=2,'prompt'=4,'enc'=4] {'prompt'}, dimensions={0}, use_global_device_ids=true | all-gather | bytes 655360 | tf_op jit(solution)/shard_map/all_gather | solution.py:144
  33.9 7.2 %all-gather.2 = f32[128,8,16]{2,1,0:T(8,128)S(1)} all-gather(f32[32,8,16]{2,1,0:T(8,128)S(1)} %copy.52), channel_id=4, replica_groups=mesh['groups'=2,'prompt'=4,'enc'=4] {'enc'}, dimensions={0}, use_global_device_ids=true | all-gather | bytes 81920 | tf_op jit(solution)/shard_map/all_gather | solution.py:18
  41.4 5.2 all-gather.4
  46.6 5.2 all-gather.3
  55.4 27.0 %reshape.331 = s32[64,2,2,64,2,2]{5,4,3,2,1,0:T(2,128)} reshape(s32[256,256]{1,0:T(8,128)S(1)} %copy-done.55) | data formatting | bytes 524288 | tf_op jit(solution)/shard_map/reshape | solution.py:49
  82.4 20.9 %copy.55 = s32[64,64,2,2,2,2]{1,0,5,4,3,2:T(8,128)S(1)} copy(s32[64,64,2,2,2,2]{5,3,1,4,2,0:T(2,128)} %bitcast.446) | data formatting | bytes 524288 | tf_op jit(solution)/shard_map/transpose | solution.py:50
  105.7 374.7 %while.36 = (s32[]{:T(128)}, f32[1024,128]{0,1:T(8,128)}, f32[1024,256]{0,1:T(8,128)}, f32[8,4,256]{2,1,0:T(4,128)}, f32[8,4,256]{2,1,0:T(4,128)}, /*index=5*/bf...) while((s32[]{:T(128)}, f32[1024,128]{0,1:T(8,128)}, ...), condition=%wide.region_18.19_spmd.clone, body=%wide.region_6.18_spmd.clone.sunk | while | flops 692868864 | bytes 118107712 | solution.py:204
  112.7 3.8 fusion.345
  116.6 5.5 multiply_multiply_fusion.19
  132.2 3.6 multiply_reduce_fusion.13
  158.6 3.8 fusion.345
  162.5 5.5 multiply_multiply_fusion.19
  205.6 3.8 fusion.345
  209.4 5.5 multiply_multiply_fusion.19
  225.0 3.6 multiply_reduce_fusion.13
  252.5 3.8 fusion.345
  256.3 5.5 multiply_multiply_fusion.19
  271.9 3.6 multiply_reduce_fusion.13
  299.4 3.8 fusion.345
  303.3 5.5 multiply_multiply_fusion.19
  318.9 3.6 multiply_reduce_fusion.13
  346.4 3.8 fusion.345
  350.2 5.5 multiply_multiply_fusion.19
  365.8 3.6 multiply_reduce_fusion.13
  393.3 3.8 fusion.345
  397.2 5.5 multiply_multiply_fusion.19
  412.8 3.6 multiply_reduce_fusion.13
  440.3 3.8 fusion.345
  444.1 5.5 multiply_multiply_fusion.19
  459.7 3.6 multiply_reduce_fusion.13
  481.2 10.9 %psum.14 = f32[32,256]{1,0:T(8,128)S(1)} all-reduce(f32[32,256]{1,0:T(8,128)S(1)} %reshape.333), channel_id=1, replica_groups=mesh['groups'=2,'prompt'=4,'enc'=4] {'enc'}, use_global_device_ids=true, to_apply=%region_19.20 | all-reduce | flops 8192 | bytes 65536 | tf_op jit(solution)/shard_map/psum | solution.py:208
  504.3 53.4 %all-reduce.3.cloned.1.call-done = f32[1024,256]{1,0:T(8,128)} async-done(((f32[1024,256]{1,0:T(8,128)}), f32[1024,256]{1,0:T(8,128)}) %all-reduce.3.cloned.1.call-update) | async-done | bytes 1048592 | tf_op jit(solution)/shard_map/psum | solution.py:228
  (1300 shorter events, 293.6 us)
Async XLA Ops:
  6.5 98.0 %copy-start = (bf16[256,128]{1,0:T(8,128)(2,1)S(1)}, bf16[256,128]{1,0:T(8,128)(2,1)}, u32[]{:S(2)}) copy-start(bf16[256,128]{1,0:T(8,128)(2,1)} %param.37) | copy-start | bytes 196612
  6.5 23.2 %copy-start.57 = (bf16[256,128]{1,0:T(8,128)(2,1)S(1)}, bf16[256,128]{1,0:T(8,128)(2,1)}, u32[]{:S(2)}) copy-start(bf16[256,128]{1,0:T(8,128)(2,1)} %param.34) | copy-start | bytes 196612
  6.5 23.5 %copy-start.59 = (bf16[256,128]{1,0:T(8,128)(2,1)S(1)}, bf16[256,128]{1,0:T(8,128)(2,1)}, u32[]{:S(2)}) copy-start(bf16[256,128]{1,0:T(8,128)(2,1)} %param.35) | copy-start | bytes 196612
  6.5 551.2 %all-reduce.3.cloned.1.call-start = ((), (), s32[]{:S(2)}) async-start(), calls=%async_computation | async-start | bytes 2097152 | tf_op jit(solution)/shard_map/psum | solution.py:228
  33.8 18.3 %copy-start.56 = (bf16[128,256]{1,0:T(8,128)(2,1)S(1)}, bf16[128,256]{1,0:T(8,128)(2,1)}, u32[]{:S(2)}) copy-start(bf16[128,256]{1,0:T(8,128)(2,1)} %param.36) | copy-start | bytes 196612
  33.8 19.2 %copy-start.70 = (f32[256]{0:T(256)S(1)}, f32[256]{0:T(256)}, u32[]{:S(2)}) copy-start(f32[256]{0:T(256)} %param.41) | copy-start | bytes 3076
  33.8 19.9 %copy-start.74 = (s32[4]{0:T(128)S(1)}, s32[4]{0:T(128)}, u32[]{:S(2)}) copy-start(s32[4]{0:T(128)} %param.29) | copy-start | bytes 52
  33.8 21.6 %copy-start.55 = (s32[256,256]{1,0:T(8,128)S(1)}, s32[256,256]{1,0:T(8,128)}, u32[]{:S(2)}) copy-start(s32[256,256]{1,0:T(8,128)} %param.30) | copy-start | bytes 786436
  52.0 30.4 %copy-start.63 = (f32[32,8]{0,1:T(8,128)}, f32[32,8]{0,1:T(8,128)S(1)}, u32[]{:S(2)}) copy-start(f32[32,8]{0,1:T(8,128)S(1)} %get-tuple-element.283) | copy-start | bytes 3076
  52.0 30.4 %copy-start.65 = (f32[32,8]{0,1:T(8,128)}, f32[32,8]{0,1:T(8,128)S(1)}, u32[]{:S(2)}) copy-start(f32[32,8]{0,1:T(8,128)S(1)} %get-tuple-element.286) | copy-start | bytes 3076
  52.0 30.4 %copy-start.52 = (f32[32,8,16]{0,2,1:T(8,128)}, f32[32,8,16]{0,2,1:T(8,128)S(1)}, u32[]{:S(2)}) copy-start(f32[32,8,16]{0,2,1:T(8,128)S(1)} %broadcast_divide_fusion) | copy-start | bytes 49156
  52.4 30.0 %copy-start.71 = (f32[32]{0:T(128)}, f32[32]{0:T(128)S(1)}, u32[]{:S(2)}) copy-start(f32[32]{0:T(128)S(1)} %broadcast_multiply_fusion.3) | copy-start | bytes 388
  52.6 29.8 %copy-start.73 = (f32[32]{0:T(128)}, f32[32]{0:T(128)S(1)}, u32[]{:S(2)}) copy-start(f32[32]{0:T(128)S(1)} %multiply_reduce_fusion.6) | copy-start | bytes 388
  53.0 29.5 %copy-start.72 = (f32[32]{0:T(128)}, f32[32]{0:T(128)S(1)}, u32[]{:S(2)}) copy-start(f32[32]{0:T(128)S(1)} %fusion.146) | copy-start | bytes 388
  116.5 5.6 copy-start.5
  116.5 6.4 %copy-start.53 = (bf16[256,32]{0,1:T(8,128)(2,1)S(1)}, bf16[256,32]{0,1:T(8,128)(2,1)}, u32[]{:S(2)}) copy-start(bf16[256,32]{0,1:T(8,128)(2,1)} %get-tuple-element.825) | copy-start | bytes 49156 | tf_op jit(solution)/shard_map/while
  141.7 6.0 %copy-start.4 = (f32[1024,256]{0,1:T(8,128)S(1)}, f32[1024,256]{0,1:T(8,128)}, u32[]{:S(2)}) copy-start(f32[1024,256]{0,1:T(8,128)} %copy-done.3) | copy-start | bytes 3145732 | tf_op jit(solution)/shard_map/while
  162.4 5.6 copy-start.5
  162.4 6.4 %copy-start.53 = (bf16[256,32]{0,1:T(8,128)(2,1)S(1)}, bf16[256,32]{0,1:T(8,128)(2,1)}, u32[]{:S(2)}) copy-start(bf16[256,32]{0,1:T(8,128)(2,1)} %get-tuple-element.825) | copy-start | bytes 49156 | tf_op jit(solution)/shard_map/while
  187.5 6.0 %copy-start.4 = (f32[1024,256]{0,1:T(8,128)S(1)}, f32[1024,256]{0,1:T(8,128)}, u32[]{:S(2)}) copy-start(f32[1024,256]{0,1:T(8,128)} %copy-done.3) | copy-start | bytes 3145732 | tf_op jit(solution)/shard_map/while
  209.4 6.5 %copy-start.53 = (bf16[256,32]{0,1:T(8,128)(2,1)S(1)}, bf16[256,32]{0,1:T(8,128)(2,1)}, u32[]{:S(2)}) copy-start(bf16[256,32]{0,1:T(8,128)(2,1)} %get-tuple-element.825) | copy-start | bytes 49156 | tf_op jit(solution)/shard_map/while
  234.5 6.0 %copy-start.4 = (f32[1024,256]{0,1:T(8,128)S(1)}, f32[1024,256]{0,1:T(8,128)}, u32[]{:S(2)}) copy-start(f32[1024,256]{0,1:T(8,128)} %copy-done.3) | copy-start | bytes 3145732 | tf_op jit(solution)/shard_map/while
  256.3 6.5 %copy-start.53 = (bf16[256,32]{0,1:T(8,128)(2,1)S(1)}, bf16[256,32]{0,1:T(8,128)(2,1)}, u32[]{:S(2)}) copy-start(bf16[256,32]{0,1:T(8,128)(2,1)} %get-tuple-element.825) | copy-start | bytes 49156 | tf_op jit(solution)/shard_map/while
  281.5 6.0 %copy-start.4 = (f32[1024,256]{0,1:T(8,128)S(1)}, f32[1024,256]{0,1:T(8,128)}, u32[]{:S(2)}) copy-start(f32[1024,256]{0,1:T(8,128)} %copy-done.3) | copy-start | bytes 3145732 | tf_op jit(solution)/shard_map/while
  303.3 6.5 %copy-start.53 = (bf16[256,32]{0,1:T(8,128)(2,1)S(1)}, bf16[256,32]{0,1:T(8,128)(2,1)}, u32[]{:S(2)}) copy-start(bf16[256,32]{0,1:T(8,128)(2,1)} %get-tuple-element.825) | copy-start | bytes 49156 | tf_op jit(solution)/shard_map/while
  328.4 6.0 %copy-start.4 = (f32[1024,256]{0,1:T(8,128)S(1)}, f32[1024,256]{0,1:T(8,128)}, u32[]{:S(2)}) copy-start(f32[1024,256]{0,1:T(8,128)} %copy-done.3) | copy-start | bytes 3145732 | tf_op jit(solution)/shard_map/while
  350.2 6.5 %copy-start.53 = (bf16[256,32]{0,1:T(8,128)(2,1)S(1)}, bf16[256,32]{0,1:T(8,128)(2,1)}, u32[]{:S(2)}) copy-start(bf16[256,32]{0,1:T(8,128)(2,1)} %get-tuple-element.825) | copy-start | bytes 49156 | tf_op jit(solution)/shard_map/while
  375.3 6.0 %copy-start.4 = (f32[1024,256]{0,1:T(8,128)S(1)}, f32[1024,256]{0,1:T(8,128)}, u32[]{:S(2)}) copy-start(f32[1024,256]{0,1:T(8,128)} %copy-done.3) | copy-start | bytes 3145732 | tf_op jit(solution)/shard_map/while
  397.2 6.4 %copy-start.53 = (bf16[256,32]{0,1:T(8,128)(2,1)S(1)}, bf16[256,32]{0,1:T(8,128)(2,1)}, u32[]{:S(2)}) copy-start(bf16[256,32]{0,1:T(8,128)(2,1)} %get-tuple-element.825) | copy-start | bytes 49156 | tf_op jit(solution)/shard_map/while
  422.3 6.0 %copy-start.4 = (f32[1024,256]{0,1:T(8,128)S(1)}, f32[1024,256]{0,1:T(8,128)}, u32[]{:S(2)}) copy-start(f32[1024,256]{0,1:T(8,128)} %copy-done.3) | copy-start | bytes 3145732 | tf_op jit(solution)/shard_map/while
  444.1 6.4 %copy-start.53 = (bf16[256,32]{0,1:T(8,128)(2,1)S(1)}, bf16[256,32]{0,1:T(8,128)(2,1)}, u32[]{:S(2)}) copy-start(bf16[256,32]{0,1:T(8,128)(2,1)} %get-tuple-element.825) | copy-start | bytes 49156 | tf_op jit(solution)/shard_map/while
  469.2 6.0 %copy-start.4 = (f32[1024,256]{0,1:T(8,128)S(1)}, f32[1024,256]{0,1:T(8,128)}, u32[]{:S(2)}) copy-start(f32[1024,256]{0,1:T(8,128)} %copy-done.3) | copy-start | bytes 3145732 | tf_op jit(solution)/shard_map/while
  (389 other events, 1025.8 us)
Sparse Core Ops, SparseCore 0:
  504.4 53.2 all-reduce.2
where the time goes:
time: 573 us; the launch traced here: 566 us
  matrix products  223 us (39%)
  other arithmetic  124 us (22%)
  local copies, waits for them, and re-layouts  95 us (17%)
  waiting for transfers between devices  53.4 us (9%)
  blocking collectives  45.8 us (8%)
  between operations  14.6 us (3%)
  loops' own time  11.1 us (2%)
    dot_general x16, matrix products, image_side(): jnp.einsum('oij,jp->oip', first_activation, second_upsample_weight, prefe...  59.2 us
    psum x1, waiting for transfers between devices, on_device(): summed = lax.psum(result, 'prompt')  53.4 us
    mul x8, other arithmetic, image_side(): jax.nn.gelu(second_result, approximate=False).reshape(row_count, 4, 4, -1)  44.4 us
    dot_general x16, matrix products, image_side(): logits = jnp.einsum('tasc,c->tas', features, hyper, precision=highest_value)  28.8 us
    reshape x1, local copies, waits for them, and re-layouts, token_pixel_scores(): grid_view = labels.reshape(side, 2, 2, side, 2, 2)  27 us
    dot_general x24, matrix products, image_side(): jnp.einsum('jhd,rhd->jhr', query_image.reshape(row_count, HEADS, HD), tok...  24.1 us
    dot_general x16, matrix products, image_side(): jnp.dot(tokens_one, wk_i.astype(jnp.float32), precision=highest_value)  23 us
    add x16, other arithmetic, single_prompt(): return ((carry[0] + d_query, carry[1] + d_image), d_tokens)  22.7 us
  transfers between devices with their start and end apart: 1, of which 1 were waited for; matrix products, arithmetic and copies ran while one was open for 0% of the time, Pallas kernels for 0%

commit v1 on v0

v1 whole, which is shorter than its diff:
```python
import functools
import math

import jax
import jax.numpy as jnp
from jax import lax
from jax.experimental import pallas as pl
from jax.experimental.pallas import tpu as pltpu
from jax.sharding import PartitionSpec as P

HEADS = 8
HD = 16
IMG = 1024
CHUNK = 16
TOK = 4 * CHUNK
COLS = 256
SCALE = HD ** (-0.5)
EPS = 1e-05
HIGH = lax.Precision.HIGHEST
F32 = jnp.float32
BF16 = jnp.bfloat16
VMEM_LIMIT = 56 * 1024 * 1024

NN = (((1,), (0,)), ((), ()))
NT = (((1,), (1,)), ((), ()))
TN = (((0,), (0,)), ((), ()))


def exact(a, b, dims=NN):
    return lax.dot_general(
        a.astype(F32), b.astype(F32), dims, precision=HIGH, preferred_element_type=F32
    )


def single(a, b, dims=NN):
    return lax.dot_general(a, b, dims, preferred_element_type=F32)


def parts(values):
    high = values.astype(BF16)
    rest = values - high.astype(F32)
    middle = rest.astype(BF16)
    low = (rest - middle.astype(F32)).astype(BF16)
    return high, middle, low


def head_mask(rows, head):
    lane = lax.broadcasted_iota(jnp.int32, (rows, 128), 1)
    return (lane // HD == head).astype(F32)


def by_head(values):
    return jnp.concatenate(
        [values * head_mask(values.shape[0], h) for h in range(HEADS)], axis=0
    )


def token_by_head(values):
    lane = lax.broadcasted_iota(jnp.int32, (1, HEADS, 128), 2)
    head = lax.broadcasted_iota(jnp.int32, (1, HEADS, 128), 1)
    mask = (lane // HD == head).astype(F32)
    return (values[:, None, :] * mask).reshape(values.shape[0] * HEADS, 128)


def fold_heads(values):
    count = values.shape[0] // HEADS
    lane = lax.broadcasted_iota(jnp.int32, (1, HEADS, 128), 2)
    head = lax.broadcasted_iota(jnp.int32, (1, HEADS, 128), 1)
    mask = (lane // HD == head).astype(F32)
    return jnp.sum(values.reshape(count, HEADS, 128) * mask, axis=1)


def prep_kernel(up, wo, w2, wv, g2, g3, up_t, wo_t, w2_t, wv_t, up3, wo3, w23, g2b, g3b):
    def turned(ref):
        return jnp.transpose(ref[...].astype(F32)).astype(BF16)

    up_t[...] = turned(up)
    wo_t[...] = turned(wo)
    w2_t[...] = turned(w2)
    wv_t[...] = turned(wv)
    for src, dst in ((up, up3), (wo, wo3), (w2, w23)):
        width = src.shape[1]
        for k in range(3):
            dst[:, k * width : (k + 1) * width] = src[...]
    for src, dst in ((g2, g2b), (g3, g3b)):
        column = jnp.transpose(jnp.broadcast_to(src[...], (128, src.shape[1])))
        for k in range(COLS // 128):
            dst[:, k * 128 : (k + 1) * 128] = column


def gather_kernel(
    nblocks,
    embed_rows,
    coded,
    rank,
    own,
    *refs,
):
    blocks = refs[:nblocks]
    (table, type_embed, fourier, wq, wk, wv, wv_t, wqi) = refs[nblocks : nblocks + 8]
    (payload, tokens, queries, live, key_own, value_own, query_t, embed_t) = refs[
        nblocks + 8 : nblocks + 16
    ]
    key_all, value_t = refs[nblocks + 16 :]
    chunk = pl.program_id(0)

    def first():
        for k in range(nblocks):
            rows = blocks[k][0:embed_rows, :]
            key_all[k * embed_rows : (k + 1) * embed_rows, :] = single(rows, wk[...])
            value_t[:, k * embed_rows : (k + 1) * embed_rows] = single(wv_t[...], rows, NT)
        mine = own[...]
        key_own[...] = single(mine, wk[...])
        value_own[...] = single(mine, wv[...])
        query_t[...] = jnp.transpose(single(mine, wqi[...]))
        embed_t[...] = jnp.transpose(mine.astype(F32))

    pl.when(chunk == 0)(first)

    if coded:
        pieces = []
        for k in range(nblocks):
            code = blocks[k][embed_rows : embed_rows + 16, 0:128].astype(F32)
            pieces.append(code[0:8] * 32.0 + code[8:16])
        slots = jnp.concatenate(pieces, axis=0)
    else:
        slots = table[...]
    slot_count = slots.shape[0]
    number = lax.broadcasted_iota(jnp.int32, (CHUNK, slot_count), 0) + chunk * CHUNK
    chosen = (number == rank[0:1, :]).astype(F32)
    rows = exact(chosen, slots)
    live[...] = rows
    scaled = 2.0 * ((rows + 0.5) / IMG) - 1.0
    two_pi = 2.0 * math.pi
    kinds = [jnp.broadcast_to(type_embed[0:1, :], (CHUNK, 256))]
    for r in range(3):
        across = scaled[:, 2 * r : 2 * r + 1] * fourier[0:1, :]
        down = scaled[:, 2 * r + 1 : 2 * r + 2] * fourier[1:2, :]
        angles = two_pi * (across + down)
        code = jnp.concatenate([jnp.sin(angles), jnp.cos(angles)], axis=-1)
        kinds.append(code + type_embed[r + 1 : r + 2, :])
    token_rows = jnp.concatenate(kinds, axis=0)
    tokens[...] = token_rows
    query_rows = exact(token_rows, wq[...])
    queries[...] = query_rows

    scores = exact(key_all[...], by_head(query_rows * SCALE), NT)
    top = jnp.max(scores, axis=0, keepdims=True)
    shifted = jnp.exp(scores - top)
    total = jnp.sum(shifted, axis=0, keepdims=True)
    gathered = exact(value_t[...], shifted)
    first_half = lax.broadcasted_iota(jnp.int32, (HD, 128), 1) < TOK
    for k in range(4):
        lanes = slice(128 * k, 128 * k + 128)
        even = gathered[32 * k : 32 * k + 16, lanes]
        odd = gathered[32 * k + 16 : 32 * k + 32, lanes]
        payload[0, HD * k : HD * k + HD, :] = jnp.where(first_half, even, odd)
        payload[0, 64 + k : 65 + k, :] = top[:, lanes]
        payload[0, 68 + k : 69 + k, :] = total[:, lanes]


def gelu_pair(x):
    phi = 0.5 + 0.5 * lax.erf(x * (0.5**0.5))
    bell = jnp.exp2(x * x * (-0.5 * math.log2(math.e)))
    return x * phi, phi + x * (bell * (1.0 / math.sqrt(2.0 * math.pi)))


def column_norm(values, count):
    centered = values - jnp.sum(values, axis=0, keepdims=True) * (1.0 / count)
    variance = jnp.sum(centered * centered, axis=0, keepdims=True) * (1.0 / count)
    inverse = lax.rsqrt(variance + EPS)
    return centered * inverse, inverse


def column_norm_pull(cotangent, normed, inverse, count):
    mean = jnp.sum(cotangent, axis=0, keepdims=True) * (1.0 / count)
    along = jnp.sum(cotangent * normed, axis=0, keepdims=True) * (1.0 / count)
    return inverse * (cotangent - mean - normed * along)


def prompt_kernel(
    senders,
    row_count,
    payload,
    tokens,
    live,
    embed_t,
    query_t,
    labels,
    wo_t,
    gain_one,
    wk_i,
    wv_i,
    wq_i,
    hyper_one,
    hyper_two,
    up_t,
    wo_i_t,
    w2_t,
    up3,
    wo3,
    w23,
    g2b,
    g3b,
    image_out,
    gathered_out,
    stat_out,
    pull_out,
    image_sum,
    score_ref,
    key_ref,
    value_ref,
    value_cat,
    score_grad,
    value_grad,
    hyper_ref,
    hyper_sum,
    target_ref,
):
    share = COLS // row_count
    blocks = CHUNK // share
    chunk = pl.program_id(0)
    lane = lax.broadcasted_iota(jnp.int32, (1, COLS), 1)

    def segment(p):
        return lane // row_count == p

    gathered_pieces = []
    half = TOK
    tops, totals = [], []
    for k in range(4):
        top = payload[0, 0, 64 + k : 65 + k, :]
        for d in range(1, senders):
            top = jnp.maximum(top, payload[d, 0, 64 + k : 65 + k, :])
        total = jnp.zeros_like(top)
        summed = jnp.zeros((HD, 128), F32)
        for d in range(senders):
            factor = jnp.exp(payload[d, 0, 64 + k : 65 + k, :] - top)
            total = total + payload[d, 0, 68 + k : 69 + k, :] * factor
            summed = summed + payload[d, 0, HD * k : HD * k + HD, :] * factor
        packed = summed / total
        gathered_pieces.append(packed[:, 0:half])
        gathered_pieces.append(packed[:, half : 2 * half])
        stat_out[0, k : k + 1, :] = top
        stat_out[0, 4 + k : 5 + k, :] = total
    gathered = jnp.transpose(jnp.concatenate(gathered_pieces, axis=0))
    gathered_out[...] = gathered

    summed = tokens[...] + exact(gathered, wo_t[...])
    centered = summed - jnp.mean(summed, axis=-1, keepdims=True)
    variance = jnp.mean(centered * centered, axis=-1, keepdims=True)
    token_inverse = lax.rsqrt(variance + EPS)
    token_normed = centered * token_inverse
    tokens_one = token_normed * gain_one[...]
    key_ref[...] = token_by_head(exact(tokens_one, wk_i[...]) * SCALE)
    value_rows = token_by_head(exact(tokens_one, wv_i[...]))
    value_ref[...] = value_rows.reshape(4, CHUNK, HEADS, 128)
    score_ref[...] = exact(key_ref[...], query_t[...]).reshape(4, CHUNK, HEADS, COLS)
    value_turned = jnp.transpose(
        jnp.transpose(value_rows.reshape(4, CHUNK, HEADS, 128), (1, 0, 2, 3)).reshape(
            CHUNK * 32, 128
        )
    )
    high, middle, low = parts(value_turned)
    for g in range(CHUNK):
        at = slice(32 * g, 32 * g + 32)
        value_cat[g] = jnp.concatenate(
            [high[:, at], high[:, at], high[:, at], middle[:, at], middle[:, at], low[:, at]],
            axis=1,
        )
    output_rows = jnp.broadcast_to(tokens_one[0:1, :], (128, 256))
    hidden = jnp.maximum(exact(output_rows, hyper_one[...]), 0.0)
    hyper_columns = jnp.transpose(exact(hidden, hyper_two[...]))
    for k in range(COLS // 128):
        hyper_ref[:, 128 * k : 128 * k + 128] = hyper_columns
    for b in range(blocks):
        row = jnp.broadcast_to(live[b * share : b * share + 1, 6:7], (1, COLS))
        for p in range(1, share):
            row = jnp.where(segment(p), live[b * share + p : b * share + p + 1, 6:7], row)
        target_ref[b] = row

    hyper_sum[...] = jnp.zeros_like(hyper_sum)

    def clear():
        image_sum[...] = jnp.zeros_like(image_sum)
        image_out[...] = jnp.zeros_like(image_out)

    pl.when(chunk == 0)(clear)

    def block(b, carry):
        base = b * share
        if share == 1:
            scores = score_ref[:, base]
        else:
            scores = score_ref[:, 0]
            for p in range(1, share):
                scores = jnp.where(segment(p), score_ref[:, p], scores)
        top = jnp.max(scores, axis=0, keepdims=True)
        raised = jnp.exp(scores - top)
        probs = raised / jnp.sum(raised, axis=0, keepdims=True)
        prob_rows = probs.reshape(32, COLS)
        ph, pm, pw = parts(prob_rows)
        stacked = jnp.concatenate([ph, pm, pw, ph, pm, ph], axis=0)
        mixed = single(value_cat[base], stacked)
        for p in range(1, share):
            mixed = jnp.where(segment(p), single(value_cat[p], stacked), mixed)
        mixed = mixed.astype(BF16)
        normed, inverse = column_norm(embed_t[...] + single(wo_i_t[...], mixed), 256)
        image_one = (normed * g2b[...]).astype(BF16)
        lifted = single(up_t[...], image_one)
        target = target_ref[b]
        lift_parts = []
        for a in range(4):
            normed3, inverse3 = column_norm(lifted[64 * a : 64 * a + 64], 64)
            act, act_slope = gelu_pair(normed3 * g3b[...])
            second = single(w2_t[...], act.astype(BF16))
            second_parts = []
            for pos in range(4):
                feature, slope = gelu_pair(second[32 * pos : 32 * pos + 32])
                logit = jnp.sum(feature * hyper_ref[...], axis=0, keepdims=True)
                truth = (labels[4 * a + pos : 4 * a + pos + 1, :] == target).astype(F32)
                d_logit = (lax.logistic(logit) - truth) * 0.25
                hyper_sum[...] += feature * d_logit
                second_parts.append(parts(hyper_ref[...] * slope * d_logit))
            stacked_second = jnp.concatenate(
                [second_parts[pos][k] for k in range(3) for pos in range(4)], axis=0
            )
            d_act = single(w23[...], stacked_second).astype(BF16).astype(F32)
            d_normed = d_act * act_slope * g3b[...]
            lift_parts.append(parts(column_norm_pull(d_normed, normed3, inverse3, 64)))
        stacked_lift = jnp.concatenate(
            [lift_parts[a][k] for k in range(3) for a in range(4)], axis=0
        )
        d_image_one = single(up3[...], stacked_lift).astype(BF16).astype(F32)
        d_sum = column_norm_pull(d_image_one * g2b[...], normed, inverse, 256)
        image_sum[...] += d_sum
        d_mixed = single(wo3[...], jnp.concatenate(parts(d_sum), axis=0)).astype(BF16)

        def for_prompt(g, prob_terms):
            value_terms = jnp.concatenate(parts(value_ref[:, g].reshape(32, 128)), axis=0)
            d_prob = single(value_terms, d_mixed)
            d_prob = d_prob[0:32] + d_prob[32:64] + d_prob[64:96]
            d_value = single(jnp.concatenate(prob_terms, axis=0), d_mixed, NT)
            d_value = d_value[0:32] + d_value[32:64] + d_value[64:96]
            value_grad[:, g] = d_value.reshape(4, HEADS, 128)
            return d_prob

        if share == 1:
            d_prob = for_prompt(base, (ph, pm, pw))
        else:
            d_prob = jnp.zeros((32, COLS), F32)
            for p in range(share):
                kept = jnp.where(segment(p), prob_rows, 0.0)
                d_prob = jnp.where(segment(p), for_prompt(p, parts(kept)), d_prob)
        d_prob = d_prob.reshape(4, HEADS, COLS)
        d_scores = probs * (d_prob - jnp.sum(probs * d_prob, axis=0, keepdims=True))
        if share == 1:
            score_grad[:, base] = d_scores
        else:
            for p in range(share):
                score_grad[:, p] = jnp.where(segment(p), d_scores, 0.0)
        return carry

    lax.fori_loop(0, blocks, block, 0)

    score_rows = score_grad[...].reshape(TOK * HEADS, COLS)
    d_query = exact(key_ref[...], score_rows, TN)
    image_out[...] += exact(wq_i[...], d_query)
    d_key = fold_heads(exact(score_rows, query_t[...], NT)) * SCALE
    d_value = fold_heads(value_grad[...].reshape(TOK * HEADS, 128))
    d_tokens = exact(d_key, wk_i[...], NT) + exact(d_value, wv_i[...], NT)
    d_hyper = exact(jnp.ones((8, COLS), F32), hyper_sum[...], NT)
    d_hidden = jnp.where(hidden[0:8] > 0.0, exact(d_hyper, hyper_two[...], NT), 0.0)
    d_output = exact(d_hidden, hyper_one[...], NT)
    row = lax.broadcasted_iota(jnp.int32, (TOK, 256), 0)
    d_tokens = d_tokens + jnp.where(row == 0, d_output[0:1, :], 0.0)
    d_normed = d_tokens * gain_one[...]
    mean = jnp.mean(d_normed, axis=-1, keepdims=True)
    along = jnp.mean(d_normed * token_normed, axis=-1, keepdims=True)
    d_summed = token_inverse * (d_normed - mean - token_normed * along)
    pull_out[...] = exact(d_summed, wo_t[...], NT)

    def finish():
        image_out[...] += image_sum[...]

    pl.when(chunk == pl.num_programs(0) - 1)(finish)


def final_kernel(
    count,
    key_own,
    value_own,
    queries,
    gathered,
    stats,
    image_grad,
    wk,
    wv,
    *refs,
):
    pulls = refs[:count]
    out = refs[count]
    key_grad, value_grad = refs[count + 1 :]
    chunk = pl.program_id(0)

    def clear():
        key_grad[...] = jnp.zeros_like(key_grad)
        value_grad[...] = jnp.zeros_like(value_grad)

    pl.when(chunk == 0)(clear)
    pull = pulls[0][...]
    for other in pulls[1:]:
        pull = pull + other[...]
    query_rows = by_head(queries[...] * SCALE)
    pull_rows = by_head(pull)
    delta = exact(jnp.ones((8, 128), F32), by_head(pull * gathered[...]), NT)[0:1, :]
    scores = exact(key_own[...], query_rows, NT)
    top = jnp.concatenate([stats[0, k : k + 1, :] for k in range(4)], axis=1)
    total = jnp.concatenate([stats[0, 4 + k : 5 + k, :] for k in range(4)], axis=1)
    probs = jnp.exp(scores - top) * (1.0 / total)
    d_probs = exact(value_own[...], pull_rows, NT)
    d_scores = probs * (d_probs - delta)
    key_grad[...] += exact(d_scores, query_rows)
    value_grad[...] += exact(probs, pull_rows)

    def finish():
        out[...] = (
            jnp.transpose(image_grad[...])
            + exact(key_grad[...], wk[...], NT)
            + exact(value_grad[...], wv[...], NT)
        )

    pl.when(chunk == pl.num_programs(0) - 1)(finish)


def whole(shape):
    return pl.BlockSpec(shape, lambda i: (0,) * len(shape))


def chunked(shape, axis=0):
    def index(i):
        return tuple(i if d == axis else 0 for d in range(len(shape)))

    return pl.BlockSpec(shape, index)


def params():
    return pltpu.CompilerParams(
        dimension_semantics=("arbitrary",), vmem_limit_bytes=VMEM_LIMIT
    )


def shape_of(shape, dtype=F32):
    return jax.ShapeDtypeStruct(shape, dtype)


def own_labels(labels, first_token, rows):
    side = labels.shape[1] // 4
    high = max(1, rows // side)
    wide = min(side, rows)
    top = first_token // side
    left = first_token % side
    piece = lax.dynamic_slice(labels, (4 * top, 4 * left), (4 * high, 4 * wide))
    piece = piece.reshape(high, 2, 2, wide, 2, 2)
    return jnp.transpose(piece, (1, 4, 2, 5, 0, 3)).reshape(16, rows)


def on_device(
    embed,
    coords,
    targets,
    counts,
    labels,
    type_embed,
    fourier,
    wq_t,
    wk_t,
    wv_t,
    wo_t,
    wq_i,
    wk_i,
    wv_i,
    wo_i,
    gain_one,
    gain_two,
    gain_three,
    up_one,
    second_upsample_weight,
    hyper_one,
    hyper_two,
):
    n_prompt = lax.axis_size("prompt")
    n_enc = lax.axis_size("enc")
    p = lax.axis_index("prompt")
    e = lax.axis_index("enc")
    rows = embed.shape[0]
    slots = coords.shape[0]
    chunks = n_prompt * slots // 2 // CHUNK
    share = COLS // rows
    direct = n_prompt == 4 and slots == 8 and rows >= 128

    table = jnp.concatenate([coords, targets[:, None]], axis=1)
    if direct:
        code = jnp.concatenate([table // 32, table % 32], axis=0).astype(BF16)
        code = jnp.pad(code, ((0, 0), (0, 256 - 7)))
        block = jnp.concatenate([embed, code], axis=0)
        blocks = [block]
        for k in range(1, 4):
            blocks.append(lax.ppermute(block, "prompt", [(i, i ^ k) for i in range(4)]))
        owners = jnp.bitwise_xor(p, jnp.arange(4, dtype=jnp.int32))
        block_rows = rows
        table_all = jnp.zeros((8, 128), F32)
    else:
        blocks = [lax.all_gather(embed, "prompt", axis=0, tiled=True)]
        table_all = lax.all_gather(table, "prompt", axis=0, tiled=True).astype(F32)
        table_all = jnp.pad(table_all, ((0, 0), (0, 128 - 7)))
        owners = jnp.arange(n_prompt, dtype=jnp.int32)
        block_rows = rows * n_prompt
    index = jnp.arange(n_prompt, dtype=jnp.int32)
    starts = jnp.sum(jnp.where(index[None, :] < owners[:, None], counts[None, :], 0), axis=1)
    sizes = jnp.sum(jnp.where(index[None, :] == owners[:, None], counts[None, :], 0), axis=1)
    slot = jnp.arange(slots, dtype=jnp.int32)[None, :]
    rank = jnp.where(slot < sizes[:, None], starts[:, None] + slot, -1)
    rank = jnp.broadcast_to(rank.reshape(1, n_prompt * slots), (8, n_prompt * slots))
    own = own_labels(labels, (p * n_enc + e) * rows, rows).astype(F32)
    if share > 1:
        own = jnp.tile(own, (1, share))

    prepared = pl.pallas_call(
        prep_kernel,
        out_shape=(
            shape_of((256, 256), BF16),
            shape_of((256, 128), BF16),
            shape_of((128, 64), BF16),
            shape_of((128, 256), BF16),
            shape_of((256, 768), BF16),
            shape_of((128, 768), BF16),
            shape_of((64, 384), BF16),
            shape_of((256, COLS)),
            shape_of((64, COLS)),
        ),
        name="prep",
    )(
        up_one,
        wo_i,
        second_upsample_weight,
        wv_t,
        gain_two.reshape(1, 256),
        gain_three.reshape(1, 64),
    )
    up_t, wo_i_t, w2_t, wv_turned, up3, wo3, w23, g2b, g3b = prepared

    all_rows = block_rows * len(blocks)
    gather_args = (
        rank,
        embed,
        *blocks,
        table_all,
        type_embed,
        fourier,
        wq_t,
        wk_t,
        wv_t,
        wv_turned,
        wq_i,
    )
    payload, tokens, queries, live, key_own, value_own, query_t, embed_t = pl.pallas_call(
        functools.partial(gather_kernel, len(blocks), block_rows, direct),
        grid=(chunks,),
        in_specs=[whole(a.shape) for a in gather_args],
        out_specs=(
            chunked((1, 72, 128)),
            chunked((TOK, 256)),
            chunked((TOK, 128)),
            chunked((CHUNK, 128)),
            whole((rows, 128)),
            whole((rows, 128)),
            whole((128, rows)),
            whole((256, rows)),
        ),
        out_shape=(
            shape_of((chunks, 72, 128)),
            shape_of((chunks * TOK, 256)),
            shape_of((chunks * TOK, 128)),
            shape_of((chunks * CHUNK, 128)),
            shape_of((rows, 128)),
            shape_of((rows, 128)),
            shape_of((128, rows)),
            shape_of((256, rows)),
        ),
        scratch_shapes=[pltpu.VMEM((all_rows, 128), F32), pltpu.VMEM((128, all_rows), F32)],
        compiler_params=params(),
        name="gather",
    )(*gather_args)

    payloads = lax.all_gather(payload, "enc")
    if share > 1:
        embed_t = jnp.tile(embed_t, (1, share))
        query_t = jnp.tile(query_t, (1, share))
    prompt_args = (
        payloads,
        tokens,
        live,
        embed_t,
        query_t,
        own,
        wo_t,
        gain_one.reshape(1, 256),
        wk_i,
        wv_i,
        wq_i,
        hyper_one,
        hyper_two,
        up_t,
        wo_i_t,
        w2_t,
        up3,
        wo3,
        w23,
        g2b,
        g3b,
    )
    prompt_specs = [whole(a.shape) for a in prompt_args]
    prompt_specs[0] = chunked((n_enc, 1, 72, 128), 1)
    prompt_specs[1] = chunked((TOK, 256))
    prompt_specs[2] = chunked((CHUNK, 128))
    image_grad, gathered, stats, pull = pl.pallas_call(
        functools.partial(prompt_kernel, n_enc, rows),
        grid=(chunks,),
        in_specs=prompt_specs,
        out_specs=(
            whole((256, COLS)),
            chunked((TOK, 128)),
            chunked((1, 8, 128)),
            chunked((TOK, 128)),
        ),
        out_shape=(
            shape_of((256, COLS)),
            shape_of((chunks * TOK, 128)),
            shape_of((chunks, 8, 128)),
            shape_of((chunks * TOK, 128)),
        ),
        scratch_shapes=[
            pltpu.VMEM((256, COLS), F32),
            pltpu.VMEM((4, CHUNK, HEADS, COLS), F32),
            pltpu.VMEM((TOK * HEADS, 128), F32),
            pltpu.VMEM((4, CHUNK, HEADS, 128), F32),
            pltpu.VMEM((CHUNK, 128, 192), BF16),
            pltpu.VMEM((4, CHUNK, HEADS, COLS), F32),
            pltpu.VMEM((4, CHUNK, HEADS, 128), F32),
            pltpu.VMEM((32, COLS), F32),
            pltpu.VMEM((32, COLS), F32),
            pltpu.VMEM((CHUNK // share, 1, COLS), F32),
        ],
        compiler_params=params(),
        name="prompts",
    )(*prompt_args)
    if share > 1:
        image_grad = jnp.sum(image_grad.reshape(256, share, rows), axis=1)

    pull = jnp.sum(lax.all_gather(pull, "enc"), axis=0)
    if n_prompt == 4:
        pulls = [pull]
        for k in range(1, 4):
            pulls.append(lax.ppermute(pull, "prompt", [(i, i ^ k) for i in range(4)]))
    else:
        pulls = [lax.psum(pull, "prompt")]

    final_args = (
        key_own,
        value_own,
        queries,
        gathered,
        stats,
        image_grad,
        wk_t,
        wv_t,
        *pulls,
    )
    final_specs = [whole(a.shape) for a in final_args]
    final_specs[2] = chunked((TOK, 128))
    final_specs[3] = chunked((TOK, 128))
    final_specs[4] = chunked((1, 8, 128))
    for k in range(len(pulls)):
        final_specs[8 + k] = chunked((TOK, 128))
    return pl.pallas_call(
        functools.partial(final_kernel, len(pulls)),
        grid=(chunks,),
        in_specs=final_specs,
        out_specs=whole((rows, 256)),
        out_shape=shape_of((rows, 256)),
        scratch_shapes=[pltpu.VMEM((rows, 128), F32), pltpu.VMEM((rows, 128), F32)],
        compiler_params=params(),
        name="final",
    )(*final_args)


def solution(mesh):
    in_specs = (
        P(("groups", "prompt", "enc"), None),
        P(("groups", "prompt"), None),
        P(("groups", "prompt")),
        P(),
        P("groups", None),
        *([P()] * 17),
    )
    out_specs = P(("groups", "prompt", "enc"), None)
    return jax.shard_map(
        on_device, mesh=mesh, in_specs=in_specs, out_specs=out_specs, check_vma=False
    )
```

time: 573 us -> 99.3 us (0.17); the launches traced: 566 us -> 98.9 us
  matrix products: 223 us -> 0 us
  other arithmetic: 124 us -> 2.02 us
  local copies, waits for them, and re-layouts: 95 us -> 6.2 us
  Pallas kernels: 0 us -> 59.1 us
  waiting for transfers between devices: 53.4 us -> 8.41 us
  blocking collectives: 45.8 us -> 12.7 us
  between operations: 14.6 us -> 0.09 us
  loops' own time: 11.1 us -> 0 us
  starting transfers between devices: 0.01 us -> 10.3 us
    dot_general x193 -> x0, matrix products: 223 us -> none  [the longest x16 59.2 us: image_side(): jnp.einsum('oij,jp->oip', first_activation, second_upsample_weight, prefe...]
    pallas_call x0 -> x4, Pallas kernels: none -> 59.1 us  [the longest x1 45.9 us: on_device(): pl.pallas_call(functools.partial(prompt_kernel, n_enc, rows), grid=(chunk...]
    psum x1 -> x0, waiting for transfers between devices: 53.4 us -> none  [on_device(): summed = lax.psum(result, 'prompt')]
    mul x9 -> x0, other arithmetic: 44.5 us -> none  [the longest x8 44.4 us: image_side(): jax.nn.gelu(second_result, approximate=False).reshape(row_count, 4, 4, -1)]
    add_any x24 -> x0, other arithmetic: 36.2 us -> none  [the longest x8 21.2 us: image_side(): jax.nn.gelu(second_result, approximate=False).reshape(row_count, 4, 4, -1)]
    reshape x22 -> x0, local copies, waits for them, and re-layouts: 35.2 us -> none  [the longest x1 27 us: token_pixel_scores(): grid_view = labels.reshape(side, 2, 2, side, 2, 2)]
    add x24 -> x0, other arithmetic: 22.8 us -> none  [the longest x16 22.7 us: single_prompt(): return ((carry[0] + d_query, carry[1] + d_image), d_tokens)]
    all_gather x4 -> x2, blocking collectives: 34.9 us -> 12.7 us  [the longest x1 6.94 us: on_device(): payloads = lax.all_gather(payload, 'enc')]
  transfers between devices with their start and end apart: 1 -> 6, of which waited for: 1 -> 3; matrix products, arithmetic and copies ran while one was open for 0% -> 5% of each run, Pallas kernels for 0% -> 2%
where the time goes in v1:
time: 99.3 us; the launch traced here: 98.9 us
  Pallas kernels  59.1 us (60%)
  blocking collectives  12.7 us (13%)
  starting transfers between devices  10.3 us (10%)
  waiting for transfers between devices  8.41 us (8%)
  local copies, waits for them, and re-layouts  6.2 us (6%)
  other arithmetic  2.02 us (2%)
    pallas_call x1, Pallas kernels, on_device(): pl.pallas_call(functools.partial(prompt_kernel, n_enc, rows), grid=(chunk...  45.9 us
    all_gather x1, blocking collectives, on_device(): payloads = lax.all_gather(payload, 'enc')  6.94 us
    pallas_call x1, Pallas kernels, on_device(): pl.pallas_call(functools.partial(gather_kernel, len(blocks), block_rows,...  6.29 us
    all_gather x1, blocking collectives, on_device(): pull = jnp.sum(lax.all_gather(pull, 'enc'), axis=0)  5.8 us
    ppermute x3, starting transfers between devices, on_device(): blocks.append(lax.ppermute(block, 'prompt', [(i, i ^ k) for i in range(4)]))  5.68 us
    pallas_call x1, Pallas kernels, on_device(): pl.pallas_call(functools.partial(final_kernel, len(pulls)), grid=(chunks,...  4.81 us
    ppermute x3, starting transfers between devices, on_device(): pulls.append(lax.ppermute(pull, 'prompt', [(i, i ^ k) for i in range(4)]))  4.64 us
    ppermute x3, waiting for transfers between devices, on_device(): pulls.append(lax.ppermute(pull, 'prompt', [(i, i ^ k) for i in range(4)]))  4.32 us
  transfers between devices with their start and end apart: 6, of which 3 were waited for; matrix products, arithmetic and copies ran while one was open for 5% of the time, Pallas kernels for 2%

profile of v1, /device:TPU:0, one launch (start us, length us, event | category | flops | bytes accessed | tf_op | source)
XLA Modules:
  0.0 98.9 jit_solution(6133415547951493754)
XLA Ops:
  0.0 0.7 copy-done.10
  0.7 0.1 copy.32
  0.7 0.1 fusion.3
  0.8 0.9 pad_maximum_fusion.refs_0_
  1.8 3.1 %collective-permute-start = (bf16[272,256]{1,0:T(8,128)(2,1)S(1)}, bf16[272,256]{1,0:T(8,128)(2,1)S(1)}, u32[]{:S(2)}, u32[]{:S(2)}) collective-permute-start(bf16[272,256]{1,0:T(8,128)(2,1)S(1)} %pad_maximum_fusion.refs_0_), channel_id=1, source_target_pairs={{0,4},{4,0},{8,12},{12,8},{1,5},{5,1},{9,13},{13,9},{2,6},{6,2},{1... | collective-permute-start | bytes 417800 | tf_op jit(solution)/shard_map/ppermute | solution.py:509
  4.9 2.6 %collective-permute-start.1 = (bf16[272,256]{1,0:T(8,128)(2,1)S(1)}, bf16[272,256]{1,0:T(8,128)(2,1)S(1)}, u32[]{:S(2)}, u32[]{:S(2)}) collective-permute-start(bf16[272,256]{1,0:T(8,128)(2,1)S(1)} %pad_maximum_fusion.refs_0_), channel_id=1, source_target_pairs={{0,8},{4,12},{8,0},{12,4},{1,9},{5,13},{9,1},{13,5},{2,10},{6,14},... | collective-permute-start | bytes 417800 | tf_op jit(solution)/shard_map/ppermute | solution.py:509
  7.4 0.0 collective-permute-start.2
  7.4 0.7 dynamic-slice_convert_fusion
  8.2 1.6 %convert_element_type.13 = f32[4,2,2,64,2,2]{5,4,3,2,1,0:T(2,128)S(1)} reshape(f32[16,256]{1,0:T(8,128)S(1)} %dynamic-slice_convert_fusion) | data formatting | bytes 32768 | tf_op jit(solution)/shard_map/convert_element_type | solution.py:525
  9.8 0.5 copy.33
  10.3 0.0 copy-start.11
  10.3 0.0 copy-start.8
  10.3 0.7 convert_element_type.15.labels
  11.0 0.2 select_reduce_fusion.1
  11.2 0.1 add_select_fusion.2
  11.3 0.1 select_n.45
  11.4 0.7 copy.34.hyper_two
  12.1 2.1 %prep.1 = (bf16[256,256]{1,0:T(8,128)(2,1)}, bf16[256,128]{1,0:T(8,128)(2,1)}, bf16[128,64]{1,0:T(8,128)(2,1)}, bf16[128,256]{1,0:T(8,128)(2,1)}, bf16[256,768]{...) custom-call(bf16[256,256]{1,0:T(8,128)(2,1)} %up.1, ...), custom_call_target="tpu_custom_call" | custom-call | tf_op jit(solution)/shard_map/prep/pallas_call | solution.py:529
  14.2 4.1 %collective-permute-done.1.refs_2_ = bf16[272,256]{1,0:T(8,128)(2,1)S(1)} collective-permute-done((bf16[272,256]{1,0:T(8,128)(2,1)S(1)}, bf16[272,256]{1,0:T(8,128)(2,1)S(1)}, u32[]{:S(2)}, u32[]{:S(2)}) %collective-permute-start.1) | collective-permute-done | bytes 139296 | tf_op jit(solution)/shard_map/ppermute | solution.py:509
  18.3 0.6 broadcast_in_dim.43.rank
  19.0 0.6 broadcast_in_dim.45.refs_4_
  19.6 6.3 %gather.1 = (f32[1,72,128]{2,1,0:T(8,128)}, f32[64,256]{1,0:T(8,128)}, f32[64,128]{1,0:T(8,128)}, f32[16,128]{1,0:T(8,128)}, f32[256,128]{1,0:T(8,128)}, /*index...) custom-call(s32[8,32]{1,0:T(8,128)} %broadcast_in_dim.43.rank, bf16[256,256]{1,0:T(8,128)(2,1)} %own.1, ...), custom_call_target="tpu_custom_call" | custom-call | tf_op jit(solution)/shard_map/gather/pallas_call | solution.py:567
  25.9 6.9 %all-gather = f32[4,72,128]{2,1,0:T(8,128)} all-gather(f32[1,72,128]{2,1,0:T(8,128)} %get-tuple-element.30), channel_id=2, replica_groups=mesh['groups'=2,'prompt'=4,'enc'=4] {'enc'}, dimensions={0}, use_global_device_ids=true | all-gather | bytes 184320 | tf_op jit(solution)/shard_map/all_gather | solution.py:596
  32.8 45.9 %prompts.1 = (f32[256,256]{1,0:T(8,128)}, f32[64,128]{1,0:T(8,128)}, f32[1,8,128]{2,1,0:T(8,128)}, f32[64,128]{1,0:T(8,128)}) custom-call(f32[4,1,72,128]{3,2,1,0:T(8,128)} %bitcast.8, f32[64,256]{1,0:T(8,128)} %get-tuple-element.31.tokens, f32[16,128]{1,0:T(8,128)} %get-tuple-element.32.live, f32[256,256]{1,0:T(8,128)} %get-tuple-element.33.embed_t, ...), custom_call_target="tpu_custom_call" | custom-call | tf_op jit(solution)/shard_map/prompts/pallas_call | solution.py:627
  78.7 5.8 %all-gather.1 = f32[256,128]{1,0:T(8,128)S(1)} all-gather(f32[64,128]{1,0:T(8,128)} %get-tuple-element.46), channel_id=3, replica_groups=mesh['groups'=2,'prompt'=4,'enc'=4] {'enc'}, dimensions={0}, use_global_device_ids=true | all-gather | bytes 163840 | tf_op jit(solution)/shard_map/all_gather | solution.py:661
  84.5 2.2 %collective-permute-start.3 = (f32[64,128]{1,0:T(8,128)S(1)}, f32[64,128]{1,0:T(8,128)S(1)}, u32[]{:S(2)}, u32[]{:S(2)}) collective-permute-start(f32[64,128]{1,0:T(8,128)S(1)} %reduce_sum.29.refs_0_), channel_id=1, source_target_pairs={{0,4},{4,0},{8,12},{12,8},{1,5},{5,1},{9,13},{13,9},{2,6},{6,2},{1... | collective-permute-start | bytes 98312 | tf_op jit(solution)/shard_map/ppermute | solution.py:665
  86.7 1.1 %collective-permute-start.4 = (f32[64,128]{1,0:T(8,128)S(1)}, f32[64,128]{1,0:T(8,128)S(1)}, u32[]{:S(2)}, u32[]{:S(2)}) collective-permute-start(f32[64,128]{1,0:T(8,128)S(1)} %reduce_sum.29.refs_0_), channel_id=1, source_target_pairs={{0,8},{4,12},{8,0},{12,4},{1,9},{5,13},{9,1},{13,5},{2,10},{6,14},... | collective-permute-start | bytes 98312 | tf_op jit(solution)/shard_map/ppermute | solution.py:665
  87.8 1.4 %collective-permute-start.5 = (f32[64,128]{1,0:T(8,128)S(1)}, f32[64,128]{1,0:T(8,128)S(1)}, u32[]{:S(2)}, u32[]{:S(2)}) collective-permute-start(f32[64,128]{1,0:T(8,128)S(1)} %reduce_sum.29.refs_0_), channel_id=1, source_target_pairs={{0,12},{4,8},{8,4},{12,0},{1,13},{5,9},{9,5},{13,1},{2,14},{6,10},... | collective-permute-start | bytes 98312 | tf_op jit(solution)/shard_map/ppermute | solution.py:665
  89.1 2.9 %collective-permute-done.4.refs_2_ = f32[64,128]{1,0:T(8,128)S(1)} collective-permute-done((f32[64,128]{1,0:T(8,128)S(1)}, f32[64,128]{1,0:T(8,128)S(1)}, u32[]{:S(2)}, u32[]{:S(2)}) %collective-permute-start.4) | collective-permute-done | bytes 32800 | tf_op jit(solution)/shard_map/ppermute | solution.py:665
  92.1 1.4 %collective-permute-done.5.refs_3_ = f32[64,128]{1,0:T(8,128)S(1)} collective-permute-done((f32[64,128]{1,0:T(8,128)S(1)}, f32[64,128]{1,0:T(8,128)S(1)}, u32[]{:S(2)}, u32[]{:S(2)}) %collective-permute-start.5) | collective-permute-done | bytes 32800 | tf_op jit(solution)/shard_map/ppermute | solution.py:665
  93.5 0.6 copy-done.7
  94.1 4.8 %final.1 = f32[256,256]{1,0:T(8,128)} custom-call(f32[256,128]{1,0:T(8,128)} %get-tuple-element.27.key_own, f32[256,128]{1,0:T(8,128)} %get-tuple-element.28.value_own, f32[64,128]{1,0:T(8,128)} %get-tuple-element.29.queries, f32[64,128]{1,0:T(8,128)} %get-tuple-element.43.gathered, f32[1,8,128]{2,1,0:T(8,128)} %get-tuple-element.44.stats, ...), custom_call_target="tpu_custom_call" | custom-call | tf_op jit(solution)/shard_map/final/pallas_call | solution.py:686
  (26 shorter events, 0.1 us)
Async XLA Ops:
  0.0 0.7 copy-start.10
  0.0 0.7 copy-start.9
  1.8 8.0 %copy-start = (bf16[272,256]{1,0:T(8,128)(2,1)}, bf16[272,256]{1,0:T(8,128)(2,1)S(1)}, u32[]{:S(2)}) copy-start(bf16[272,256]{1,0:T(8,128)(2,1)S(1)} %pad_maximum_fusion.refs_0_) | copy-start | bytes 417796
  1.8 12.5 %collective-permute-start = (bf16[272,256]{1,0:T(8,128)(2,1)S(1)}, bf16[272,256]{1,0:T(8,128)(2,1)S(1)}, u32[]{:S(2)}, u32[]{:S(2)}) collective-permute-start(bf16[272,256]{1,0:T(8,128)(2,1)S(1)} %pad_maximum_fusion.refs_0_), channel_id=1, source_target_pairs={{0,4},{4,0},{8,12},{12,8},{1,5},{5,1},{9,13},{13,9},{2,6},{6,2},{1... | collective-permute-start | bytes 417800 | tf_op jit(solution)/shard_map/ppermute | solution.py:509
  4.9 13.5 %collective-permute-start.1 = (bf16[272,256]{1,0:T(8,128)(2,1)S(1)}, bf16[272,256]{1,0:T(8,128)(2,1)S(1)}, u32[]{:S(2)}, u32[]{:S(2)}) collective-permute-start(bf16[272,256]{1,0:T(8,128)(2,1)S(1)} %pad_maximum_fusion.refs_0_), channel_id=1, source_target_pairs={{0,8},{4,12},{8,0},{12,4},{1,9},{5,13},{9,1},{13,5},{2,10},{6,14},... | collective-permute-start | bytes 417800 | tf_op jit(solution)/shard_map/ppermute | solution.py:509
  7.4 10.9 %collective-permute-start.2 = (bf16[272,256]{1,0:T(8,128)(2,1)S(1)}, bf16[272,256]{1,0:T(8,128)(2,1)S(1)}, u32[]{:S(2)}, u32[]{:S(2)}) collective-permute-start(bf16[272,256]{1,0:T(8,128)(2,1)S(1)} %pad_maximum_fusion.refs_0_), channel_id=1, source_target_pairs={{0,12},{4,8},{8,4},{12,0},{1,13},{5,9},{9,5},{13,1},{2,14},{6,10},... | collective-permute-start | bytes 417800 | tf_op jit(solution)/shard_map/ppermute | solution.py:509
  10.3 0.7 copy-start.11
  10.3 1.0 %copy-start.8 = (bf16[256,32]{0,1:T(8,128)(2,1)S(1)}, bf16[256,32]{0,1:T(8,128)(2,1)}, u32[]{:S(2)}) copy-start(bf16[256,32]{0,1:T(8,128)(2,1)} %param.43) | copy-start | bytes 49156
  14.2 5.3 %copy-start.1 = (bf16[272,256]{1,0:T(8,128)(2,1)}, bf16[272,256]{1,0:T(8,128)(2,1)S(1)}, u32[]{:S(2)}) copy-start(bf16[272,256]{1,0:T(8,128)(2,1)S(1)} %collective-permute-done.refs_1_) | copy-start | bytes 417796
  18.3 1.2 %copy-start.2 = (bf16[272,256]{1,0:T(8,128)(2,1)}, bf16[272,256]{1,0:T(8,128)(2,1)S(1)}, u32[]{:S(2)}) copy-start(bf16[272,256]{1,0:T(8,128)(2,1)S(1)} %collective-permute-done.1.refs_2_) | copy-start | bytes 417796
  18.3 1.2 %copy-start.3 = (bf16[272,256]{1,0:T(8,128)(2,1)}, bf16[272,256]{1,0:T(8,128)(2,1)S(1)}, u32[]{:S(2)}) copy-start(bf16[272,256]{1,0:T(8,128)(2,1)S(1)} %collective-permute-done.2.refs_3_) | copy-start | bytes 417796
  84.5 9.0 %copy-start.4 = (f32[64,128]{1,0:T(8,128)}, f32[64,128]{1,0:T(8,128)S(1)}, u32[]{:S(2)}) copy-start(f32[64,128]{1,0:T(8,128)S(1)} %reduce_sum.29.refs_0_) | copy-start | bytes 98308
  84.5 4.6 %collective-permute-start.3 = (f32[64,128]{1,0:T(8,128)S(1)}, f32[64,128]{1,0:T(8,128)S(1)}, u32[]{:S(2)}, u32[]{:S(2)}) collective-permute-start(f32[64,128]{1,0:T(8,128)S(1)} %reduce_sum.29.refs_0_), channel_id=1, source_target_pairs={{0,4},{4,0},{8,12},{12,8},{1,5},{5,1},{9,13},{13,9},{2,6},{6,2},{1... | collective-permute-start | bytes 98312 | tf_op jit(solution)/shard_map/ppermute | solution.py:665
  86.7 5.4 %collective-permute-start.4 = (f32[64,128]{1,0:T(8,128)S(1)}, f32[64,128]{1,0:T(8,128)S(1)}, u32[]{:S(2)}, u32[]{:S(2)}) collective-permute-start(f32[64,128]{1,0:T(8,128)S(1)} %reduce_sum.29.refs_0_), channel_id=1, source_target_pairs={{0,8},{4,12},{8,0},{12,4},{1,9},{5,13},{9,1},{13,5},{2,10},{6,14},... | collective-permute-start | bytes 98312 | tf_op jit(solution)/shard_map/ppermute | solution.py:665
  87.8 5.7 %collective-permute-start.5 = (f32[64,128]{1,0:T(8,128)S(1)}, f32[64,128]{1,0:T(8,128)S(1)}, u32[]{:S(2)}, u32[]{:S(2)}) collective-permute-start(f32[64,128]{1,0:T(8,128)S(1)} %reduce_sum.29.refs_0_), channel_id=1, source_target_pairs={{0,12},{4,8},{8,4},{12,0},{1,13},{5,9},{9,5},{13,1},{2,14},{6,10},... | collective-permute-start | bytes 98312 | tf_op jit(solution)/shard_map/ppermute | solution.py:665
  89.1 4.3 %copy-start.5 = (f32[64,128]{1,0:T(8,128)}, f32[64,128]{1,0:T(8,128)S(1)}, u32[]{:S(2)}) copy-start(f32[64,128]{1,0:T(8,128)S(1)} %collective-permute-done.3.refs_1_) | copy-start | bytes 98308
  92.1 1.4 %copy-start.6 = (f32[64,128]{1,0:T(8,128)}, f32[64,128]{1,0:T(8,128)S(1)}, u32[]{:S(2)}) copy-start(f32[64,128]{1,0:T(8,128)S(1)} %collective-permute-done.4.refs_2_) | copy-start | bytes 98308
  93.5 0.6 copy-start.7
